TPU v7x, 256 devices: a whole 4x4x8 slice. The times are simulated.
256 devices in a mesh: sec: 64 (over z, y, core), slab: 4 (over x).
Axes of the slice: x: 4, y: 4, z: 8, core: 2. Of those that a mesh axis runs over, the one named last changes fastest.
Arguments:
- basis: bfloat16 [128, 1024, 1024], P('sec'), may hold values from -0.1875 to 0.1875
- fermion: bfloat16 [3, 128, 1024, 1024], P(None, 'sec', None, 'slab'), may hold values from -6 to 6
- partner: int32 [3, 128], P(None, 'sec'), may hold values from 0 to 127, as said below
Outputs:
- rotated: bfloat16 [3, 128, 1024, 1024], P(None, 'sec', 'slab')
Inputs may be any that keep to these rules, and one draw needn't show every extreme that they name: partner[f, Q] // 2 equals Q // 2 or (Q // 2 + 1) % 64, so a partner lies in the block of 2 sectors that holds Q or in the next block, the last block's next being the first.
All inputs are finite; a program needn't handle non-finite values.
Results may differ from a plain program's by a relative error of at most 0.0049.
Values may be sent and summed in bfloat16 or wider, within the bound.
A program may use at most 64 MiB of HBM per device.

v0:
```python
import jax
import jax.numpy as jnp
from jax import lax
from jax.sharding import PartitionSpec as P


def shifted(block, axis, distance):
    devices = range(lax.axis_size(axis))
    route = [((i - distance) % len(devices), i) for i in devices]
    return lax.ppermute(block, axis, route)


def left_product(left_block, right_block):
    return lax.dot_general(
        left_block, right_block, (((0,), (0,)), ((), ())), preferred_element_type=jnp.float32
    ).astype(jnp.bfloat16)


def local(basis, fermion, partner):
    sectors_here = basis.shape[0]
    flavours = fermion.shape[0]
    all_sectors = sectors_here * lax.axis_size("sec")
    first_sector = lax.axis_index("sec") * sectors_here
    following = shifted(basis, "sec", -1)
    half_blocks = []
    for flavour in range(flavours):
        per_sector = []
        for sector in range(sectors_here):
            per_sector.append(left_product(basis[sector], fermion[flavour, sector]))
        half_blocks.append(jnp.stack(per_sector))
    half_rotated = jnp.stack(half_blocks)
    row_slabs = lax.all_to_all(half_rotated, "slab", split_axis=2, concat_axis=3, tiled=True)
    local_index = (partner - first_sector) % all_sectors
    out_blocks = []
    for flavour in range(flavours):
        per_sector = []
        for sector in range(sectors_here):
            where_index = local_index[flavour, sector]
            rows_here = row_slabs[flavour, sector]

            def from_own(operand):
                chosen = lax.dynamic_index_in_dim(
                    basis, jnp.minimum(where_index, sectors_here - 1), 0, keepdims=False
                )
                return jnp.dot(operand, chosen, preferred_element_type=jnp.float32)

            def from_next(operand):
                chosen = lax.dynamic_index_in_dim(
                    following, jnp.maximum(where_index - sectors_here, 0), 0, keepdims=False
                )
                return jnp.dot(operand, chosen, preferred_element_type=jnp.float32)

            product = lax.cond(where_index < sectors_here, from_own, from_next, rows_here)
            per_sector.append(product.astype(jnp.bfloat16))
        out_blocks.append(jnp.stack(per_sector))
    return jnp.stack(out_blocks)


def solution(mesh):
    placed = (P("sec", None, None), P(None, "sec", None, "slab"), P(None, "sec"))
    return jax.shard_map(
        local, mesh=mesh, in_specs=placed, out_specs=P(None, "sec", "slab", None), check_vma=False
    )
```

profile of v0, /device:TPU:88, one launch (start us, length us, event | category | flops | bytes accessed | tf_op | source)
XLA Modules:
  0.0 91.9 jit_solution(14583612871458534378)
XLA Ops:
  0.2 2.6 %fusion.159 = bf16[1,1024,256]{2,1,0:T(8,128)(2,1)S(1)} fusion(bf16[2,1024,1024]{2,1,0:T(8,128)(2,1)} %param.15, bf16[3,2,1024,256]{3,2,1,0:T(8,128)(2,1)} %param.16), kind=kOutput, calls=%fused_computation.99 | convolution fusion | flops 537133056 | bytes 3145728 | tf_op jit(solution)/shard_map/dot_general | solution.py:14
  3.0 1.0 %copy-done.6 = bf16[3,2,1024,256]{3,2,1,0:T(8,128)(2,1)S(1)} copy-done((bf16[3,2,1024,256]{3,2,1,0:T(8,128)(2,1)S(1)}, bf16[3,2,1024,256]{3,2,1,0:T(8,128)(2,1)}, u32[]{:S(2)}) %copy-start.6) | copy-done | bytes 3145752
  4.0 0.8 fusion.156
  4.7 0.8 fusion.165
  5.6 0.8 fusion.162
  6.4 0.8 fusion.168
  7.2 0.8 fusion.171
  8.2 0.3 pad_maximum_fusion
  8.5 4.9 %copy.11 = bf16[3,2,1024,256]{3,1,0,2:T(2,128)(2,1)} copy(bf16[3,2,1024,256]{3,2,1,0:T(8,128)(2,1)S(1)} %pad_maximum_fusion) | data formatting | bytes 6291456 | tf_op jit(solution)/shard_map/stack | solution.py:31
  13.4 4.4 %all-to-all-start = ((bf16[3,2,1024,256]{3,1,0,2:T(2,128)(2,1)}), bf16[3,2,1024,256]{3,1,0,2:T(2,128)(2,1)S(1)}, u32[]{:S(2)}, u32[]{:S(2)}) async-start(bf16[3,2,1024,256]{3,1,0,2:T(2,128)(2,1)} %copy.11), calls=%async_computation | async-start | bytes 6291456 | tf_op jit(solution)/shard_map/all_to_all | solution.py:32
  17.9 0.7 fusion.187
  22.3 33.1 %all-to-all-done = bf16[3,2,1024,256]{3,1,0,2:T(2,128)(2,1)S(1)} async-done(((bf16[3,2,1024,256]{3,1,0,2:T(2,128)(2,1)}), bf16[3,2,1024,256]{3,1,0,2:T(2,128)(2,1)S(1)}, u32[]{:S(2)}, u32[]{:S(2)}) %all-to-all-start) | async-done | bytes 3145760 | tf_op jit(solution)/shard_map/all_to_all | solution.py:32
  55.4 4.1 %copy.12 = bf16[3,2,256,4,256]{4,3,2,1,0:T(4,128)(2,1)} copy(bf16[3,2,256,4,256]{4,1,0,2,3:T(2,128)(2,1)S(1)} %bitcast.245) | data formatting | bytes 6291456 | tf_op jit(solution)/shard_map/all_to_all | solution.py:32
  59.5 4.7 %all_to_all.16 = bf16[3,2,256,1024]{3,2,1,0:T(8,128)(2,1)S(1)} reshape(bf16[3,2,256,4,256]{4,3,2,1,0:T(4,128)(2,1)} %copy.12) | data formatting | bytes 6291456 | tf_op jit(solution)/shard_map/all_to_all | solution.py:32
  64.2 1.7 %slice_bitcast_fusion.5 = (bf16[256,1024]{1,0:T(8,128)(2,1)}, bf16[256,1024]{1,0:T(8,128)(2,1)}, bf16[256,1024]{1,0:T(8,128)(2,1)}, bf16[256,1024]{1,0:T(8,128)(...) fusion(bf16[3,2,256,1024]{3,2,1,0:T(8,128)(2,1)S(1)} %all_to_all.16), kind=kLoop, calls=%fused_computation.115 | loop fusion | bytes 6291456 | tf_op jit(solution)/shard_map/squeeze | solution.py:39
  65.9 3.3 %conditional.6 = (bf16[1,256,1024]{2,1,0:T(8,128)(2,1)S(1)}) conditional(s32[]{:T(128)} %convert_element_type.114, (s32[]{:T(128)}, bf16[2,1024,1024]{2,1,0:T(8,128)(2,1)}, bf16[256,1024]{1,0:T(8,128)(2,1)}) %tuple.53, (s32[]{:T(128)}, bf16[2,1024,1024]{2,1,0:T(8,128)(2,1)}, bf16[256,1024]{1,0:T(8,128)(2,1)}) %tuple.54), branch_computations={%region_0.1_spmd, %region_1.2_spmd} | conditional | flops 537133056 | bytes 4194362 | solution.py:53
  66.6 2.4 %fusion.6 = bf16[1,256,1024]{1,2,0:T(8,128)(2,1)S(1)} fusion(bf16[256,1024]{1,0:T(8,128)(2,1)} %get-tuple-element.103, bf16[2,1024,1024]{2,1,0:T(8,128)(2,1)} %get-tuple-element.101, s32[]{:T(128)S(6)} %max.12), kind=kOutput, calls=%fused_computation.4 | convolution fusion | flops 537133056 | bytes 3145732 | tf_op jit(solution)/shard_map/cond/branch_0_fun/dot_general | solution.py:51
  69.1 0.2 copy.19
  69.3 3.3 %conditional.7 = (bf16[1,256,1024]{2,1,0:T(8,128)(2,1)S(1)}) conditional(s32[]{:T(128)} %convert_element_type.121, (s32[]{:T(128)}, bf16[2,1024,1024]{2,1,0:T(8,128)(2,1)}, bf16[256,1024]{1,0:T(8,128)(2,1)S(1)}) %tuple.106, (s32[]{:T(128)}, bf16[2,1024,1024]{2,1,0:T(8,128)(2,1)}, bf16[256,1024]{1,0:T(8,128)(2,1)S(1)}) %tuple.107), branch_computations={%region_2.3_spmd, %region_3.4_spmd} | conditional | flops 537133056 | bytes 4194362 | solution.py:53
  70.0 2.4 %fusion.26 = bf16[1,256,1024]{1,2,0:T(8,128)(2,1)S(1)} fusion(bf16[256,1024]{1,0:T(8,128)(2,1)S(1)} %get-tuple-element.109, bf16[2,1024,1024]{2,1,0:T(8,128)(2,1)} %get-tuple-element.107, s32[]{:T(128)S(6)} %max.13), kind=kOutput, calls=%fused_computation.16 | convolution fusion | flops 537133056 | bytes 3145732 | tf_op jit(solution)/shard_map/cond/branch_0_fun/dot_general | solution.py:51
  72.4 0.2 copy.21
  72.7 3.3 %conditional.8 = (bf16[1,256,1024]{2,1,0:T(8,128)(2,1)S(1)}) conditional(s32[]{:T(128)} %convert_element_type.122, (s32[]{:T(128)}, bf16[2,1024,1024]{2,1,0:T(8,128)(2,1)}, bf16[256,1024]{1,0:T(8,128)(2,1)S(1)}) %tuple.104, (s32[]{:T(128)}, bf16[2,1024,1024]{2,1,0:T(8,128)(2,1)}, bf16[256,1024]{1,0:T(8,128)(2,1)S(1)}) %tuple.105), branch_computations={%region_4.5_spmd, %region_5.6_spmd} | conditional | flops 537133056 | bytes 4194362 | solution.py:53
  73.5 2.4 %fusion.56 = bf16[1,256,1024]{1,2,0:T(8,128)(2,1)S(1)} fusion(bf16[256,1024]{1,0:T(8,128)(2,1)S(1)} %get-tuple-element.118, bf16[2,1024,1024]{2,1,0:T(8,128)(2,1)} %get-tuple-element.116, s32[]{:T(128)S(6)} %select_n.27), kind=kOutput, calls=%fused_computation.34 | convolution fusion | flops 537133056 | bytes 3145732 | tf_op jit(solution)/shard_map/cond/branch_1_fun/dot_general | solution.py:45
  76.1 3.2 %conditional.9 = (bf16[1,256,1024]{2,1,0:T(8,128)(2,1)S(1)}) conditional(s32[]{:T(128)} %convert_element_type.123, (s32[]{:T(128)}, bf16[2,1024,1024]{2,1,0:T(8,128)(2,1)}, bf16[256,1024]{1,0:T(8,128)(2,1)S(1)}) %tuple.102, (s32[]{:T(128)}, bf16[2,1024,1024]{2,1,0:T(8,128)(2,1)}, bf16[256,1024]{1,0:T(8,128)(2,1)S(1)}) %tuple.103), branch_computations={%region_6.7_spmd, %region_7.8_spmd} | conditional | flops 537133056 | bytes 4194362 | solution.py:53
  76.6 2.4 %fusion.66 = bf16[1,256,1024]{1,2,0:T(8,128)(2,1)S(1)} fusion(bf16[256,1024]{1,0:T(8,128)(2,1)S(1)} %get-tuple-element.121, bf16[2,1024,1024]{2,1,0:T(8,128)(2,1)} %get-tuple-element.119, s32[]{:T(128)S(6)} %max.15), kind=kOutput, calls=%fused_computation.40 | convolution fusion | flops 537133056 | bytes 3145732 | tf_op jit(solution)/shard_map/cond/branch_0_fun/dot_general | solution.py:51
  79.3 5.4 %conditional.10 = (bf16[1,256,1024]{2,1,0:T(8,128)(2,1)S(1)}) conditional(s32[]{:T(128)} %convert_element_type.124, (s32[]{:T(128)}, bf16[2,1024,1024]{2,1,0:T(8,128)(2,1)}, bf16[256,1024]{1,0:T(8,128)(2,1)}) %tuple.61, (s32[]{:T(128)}, bf16[2,1024,1024]{2,1,0:T(8,128)(2,1)}, bf16[256,1024]{1,0:T(8,128)(2,1)}) %tuple.62), branch_computations={%region_8.9_spmd, %region_9.10_spmd} | conditional | flops 537133056 | bytes 4194362 | solution.py:53
  80.3 3.2 %fusion.96 = bf16[1,256,1024]{1,2,0:T(8,128)(2,1)} fusion(bf16[256,1024]{1,0:T(8,128)(2,1)} %get-tuple-element.130, bf16[2,1024,1024]{2,1,0:T(8,128)(2,1)} %get-tuple-element.128, s32[]{:T(128)S(6)} %select_n.29), kind=kOutput, calls=%fused_computation.58 | convolution fusion | flops 537133056 | bytes 3145732 | tf_op jit(solution)/shard_map/cond/branch_1_fun/dot_general | solution.py:45
  83.5 1.2 %copy.28 = bf16[1,256,1024]{2,1,0:T(8,128)(2,1)S(1)} copy(bf16[1,256,1024]{1,2,0:T(8,128)(2,1)} %fusion.96) | data formatting | bytes 1048576 | tf_op jit(solution)/shard_map/cond | solution.py:53
  84.8 5.0 %conditional.11 = (bf16[1,256,1024]{2,1,0:T(8,128)(2,1)S(1)}) conditional(s32[]{:T(128)} %convert_element_type.125, (s32[]{:T(128)}, bf16[2,1024,1024]{2,1,0:T(8,128)(2,1)}, bf16[256,1024]{1,0:T(8,128)(2,1)S(1)}) %tuple.100, (s32[]{:T(128)}, bf16[2,1024,1024]{2,1,0:T(8,128)(2,1)}, bf16[256,1024]{1,0:T(8,128)(2,1)S(1)}) %tuple.101), branch_computations={%region_10.11_spmd, %region_11.12_spmd} | conditional | flops 537133056 | bytes 4194362 | solution.py:53
  85.3 3.2 %fusion.106 = bf16[1,256,1024]{1,2,0:T(8,128)(2,1)} fusion(bf16[256,1024]{1,0:T(8,128)(2,1)S(1)} %get-tuple-element.133, bf16[2,1024,1024]{2,1,0:T(8,128)(2,1)} %get-tuple-element.131, s32[]{:T(128)S(6)} %max.17), kind=kOutput, calls=%fused_computation.64 | convolution fusion | flops 537133056 | bytes 3145732 | tf_op jit(solution)/shard_map/cond/branch_0_fun/dot_general | solution.py:51
  88.5 1.2 %copy.29 = bf16[1,256,1024]{2,1,0:T(8,128)(2,1)S(1)} copy(bf16[1,256,1024]{1,2,0:T(8,128)(2,1)} %fusion.106) | data formatting | bytes 1048576 | tf_op jit(solution)/shard_map/cond | solution.py:53
  89.9 2.0 %pad_maximum_fusion.1 = bf16[3,2,256,1024]{3,2,1,0:T(8,128)(2,1)} fusion(bf16[1,2,256,1024]{3,2,1,0:T(8,128)(2,1)S(1)} %maximum_bitcast_fusion.5, bf16[1,2,256,1024]{3,2,1,0:T(8,128)(2,1)S(1)} %maximum_bitcast_fusion.4, bf16[1,2,256,1024]{3,2,1,0:T(8,128)(2,1)S(1)} %maximum_bitcast_fusion.3), kind=kLoop, calls=%fused_computation.73 | loop fusion | flops 3145728 | bytes 6291456 | tf_op jit(solution)/shard_map/stack | solution.py:56
  (23 shorter events, 1.4 us)
Async XLA Ops:
  0.0 3.0 %copy-start.5 = (bf16[2,1024,1024]{2,1,0:T(8,128)(2,1)S(1)}, bf16[2,1024,1024]{2,1,0:T(8,128)(2,1)}, u32[]{:S(2)}) copy-start(bf16[2,1024,1024]{2,1,0:T(8,128)(2,1)} %param.15) | copy-start | bytes 12582916
  0.0 4.0 %copy-start.6 = (bf16[3,2,1024,256]{3,2,1,0:T(8,128)(2,1)S(1)}, bf16[3,2,1024,256]{3,2,1,0:T(8,128)(2,1)}, u32[]{:S(2)}) copy-start(bf16[3,2,1024,256]{3,2,1,0:T(8,128)(2,1)} %param.16) | copy-start | bytes 9437188
  0.0 65.9 %collective-permute-start = (bf16[2,1024,1024]{2,1,0:T(8,128)(2,1)}, bf16[2,1024,1024]{2,1,0:T(8,128)(2,1)}, u32[]{:S(2)}, u32[]{:S(2)}) collective-permute-start(bf16[2,1024,1024]{2,1,0:T(8,128)(2,1)} %param.15), channel_id=1, source_target_pairs={{4,0},{8,4},{12,8},{16,12},{20,16},{24,20},{28,24},{32,28},{36,32}... | collective-permute-start | bytes 12582920 | tf_op jit(solution)/shard_map/ppermute | solution.py:10
  13.4 4.4 %copy-start.4 = (s32[3,2]{0,1:T(2,128)S(1)}, s32[3,2]{0,1:T(2,128)}, u32[]{:S(2)}) copy-start(s32[3,2]{0,1:T(2,128)} %param.17) | copy-start | bytes 76
  13.4 42.0 %all-to-all-start = ((bf16[3,2,1024,256]{3,1,0,2:T(2,128)(2,1)}), bf16[3,2,1024,256]{3,1,0,2:T(2,128)(2,1)S(1)}, u32[]{:S(2)}, u32[]{:S(2)}) async-start(bf16[3,2,1024,256]{3,1,0,2:T(2,128)(2,1)} %copy.11), calls=%async_computation | async-start | bytes 6291456 | tf_op jit(solution)/shard_map/all_to_all | solution.py:32
  65.9 3.4 %copy-start.3 = (bf16[256,1024]{1,0:T(8,128)(2,1)S(1)}, bf16[256,1024]{1,0:T(8,128)(2,1)}, u32[]{:S(2)}) copy-start(bf16[256,1024]{1,0:T(8,128)(2,1)} %get-tuple-element.148) | copy-start | bytes 1572868
  69.3 3.4 %copy-start.2 = (bf16[256,1024]{1,0:T(8,128)(2,1)S(1)}, bf16[256,1024]{1,0:T(8,128)(2,1)}, u32[]{:S(2)}) copy-start(bf16[256,1024]{1,0:T(8,128)(2,1)} %get-tuple-element.147) | copy-start | bytes 1572868
  72.7 3.3 %copy-start.1 = (bf16[256,1024]{1,0:T(8,128)(2,1)S(1)}, bf16[256,1024]{1,0:T(8,128)(2,1)}, u32[]{:S(2)}) copy-start(bf16[256,1024]{1,0:T(8,128)(2,1)} %get-tuple-element.146) | copy-start | bytes 1572868
  79.3 5.4 %copy-start = (bf16[256,1024]{1,0:T(8,128)(2,1)S(1)}, bf16[256,1024]{1,0:T(8,128)(2,1)}, u32[]{:S(2)}) copy-start(bf16[256,1024]{1,0:T(8,128)(2,1)} %get-tuple-element.144) | copy-start | bytes 1572868
where the time goes:
time: 92.5 us; the launch traced here: 91.9 us
  waiting for transfers between devices  33.1 us (36%)
  matrix products  22.4 us (24%)
  local copies, waits for them, and re-layouts  20.6 us (22%)
  starting transfers between devices  4.61 us (5%)
  loops' own time  4.29 us (5%)
  between operations  3.95 us (4%)
  other arithmetic  2.94 us (3%)
    all_to_all x1, waiting for transfers between devices, local(): lax.all_to_all(half_rotated, 'slab', split_axis=2, concat_axis=3, tiled=T...  33.1 us
    dot_general x4, matrix products, from_next(): return jnp.dot(operand, chosen, preferred_element_type=jnp.float32)  10.3 us
    all_to_all x2, local copies, waits for them, and re-layouts, local(): lax.all_to_all(half_rotated, 'slab', split_axis=2, concat_axis=3, tiled=T...  8.77 us
    dot_general x6, matrix products, left_product(): lax.dot_general(left_block, right_block, (((0,), (0,)), ((), ())), prefer...  6.49 us
    dot_general x2, matrix products, from_own(): return jnp.dot(operand, chosen, preferred_element_type=jnp.float32)  5.59 us
    another operation x1, local copies, waits for them, and re-layouts, local(): half_rotated = jnp.stack(half_blocks)  4.9 us
    all_to_all x1, starting transfers between devices, local(): lax.all_to_all(half_rotated, 'slab', split_axis=2, concat_axis=3, tiled=T...  4.43 us
    another operation x6, loops' own time, local(): lax.cond(where_index < sectors_here, from_own, from_next, rows_here)  4.29 us
  transfers between devices with their start and end apart: 2, of which 1 were waited for; matrix products, arithmetic and copies ran while one was open for 20% of the time, Pallas kernels for 0%

commit v1 on v0

--- a/solution.py
+++ b/solution.py
@@ -2,6 +2,13 @@
 import jax.numpy as jnp
 from jax import lax
 from jax.sharding import PartitionSpec as P
+
+
+def exchange_blocks(array, name, split, join):
+    size = lax.axis_size(name)
+    shards = jnp.stack(jnp.split(array, size, axis=split), axis=0)
+    shards = lax.all_to_all(shards, name, split_axis=0, concat_axis=0)
+    return jnp.concatenate(shards, axis=join)
 
 
 def shifted(block, axis, distance):
@@ -29,7 +36,7 @@
             per_sector.append(left_product(basis[sector], fermion[flavour, sector]))
         half_blocks.append(jnp.stack(per_sector))
     half_rotated = jnp.stack(half_blocks)
-    row_slabs = lax.all_to_all(half_rotated, "slab", split_axis=2, concat_axis=3, tiled=True)
+    row_slabs = exchange_blocks(half_rotated, "slab", 2, 3)
     local_index = (partner - first_sector) % all_sectors
     out_blocks = []
     for flavour in range(flavours):

time: 92.5 us -> 84.6 us (0.915)
  local copies, waits for them, and re-layouts: 20.6 us -> 11.2 us
  other arithmetic: 2.94 us -> 4.82 us
    all_to_all x2 -> x0, local copies, waits for them, and re-layouts: 8.77 us -> none  [local(): lax.all_to_all(half_rotated, 'slab', split_axis=2, concat_axis=3, tiled=T...]
    another operation x1, local copies, waits for them, and re-layouts: 4.9 us -> 0.21 us  [exchange_blocks(): shards = jnp.stack(jnp.split(array, size, axis=split), axis=0)]
    reshape x0 -> x1, local copies, waits for them, and re-layouts: none -> 2.76 us  [exchange_blocks(): return jnp.concatenate(shards, axis=join)]
    another operation x0 -> x1, other arithmetic: none -> 1.88 us  [exchange_blocks(): shards = jnp.stack(jnp.split(array, size, axis=split), axis=0)]
    squeeze x1, local copies, waits for them, and re-layouts: 1.71 us -> 3.05 us  [local(): rows_here = row_slabs[flavour, sector]]
  transfers between devices with their start and end apart: 2 -> 2, of which waited for: 1 -> 1; matrix products, arithmetic and copies ran while one was open for 20% -> 19% of each run, Pallas kernels for 0% -> 0%
where the time goes in v1:
time: 84.6 us; the launch traced here: 84 us
  waiting for transfers between devices  33.2 us (39%)
  matrix products  22.3 us (26%)
  local copies, waits for them, and re-layouts  11.2 us (13%)
  other arithmetic  4.82 us (6%)
  starting transfers between devices  4.61 us (5%)
  loops' own time  4.04 us (5%)
  between operations  3.81 us (5%)
    all_to_all x1, waiting for transfers between devices, exchange_blocks(): shards = lax.all_to_all(shards, name, split_axis=0, concat_axis=0)  33.2 us
    dot_general x4, matrix products, from_next(): return jnp.dot(operand, chosen, preferred_element_type=jnp.float32)  10.2 us
    dot_general x6, matrix products, left_product(): lax.dot_general(left_block, right_block, (((0,), (0,)), ((), ())), prefer...  6.49 us
    dot_general x2, matrix products, from_own(): return jnp.dot(operand, chosen, preferred_element_type=jnp.float32)  5.59 us
    all_to_all x1, starting transfers between devices, exchange_blocks(): shards = lax.all_to_all(shards, name, split_axis=0, concat_axis=0)  4.42 us
    another operation x6, loops' own time, local(): lax.cond(where_index < sectors_here, from_own, from_next, rows_here)  4.04 us
    cond x6, local copies, waits for them, and re-layouts, local(): lax.cond(where_index < sectors_here, from_own, from_next, rows_here)  3.31 us
    squeeze x1, local copies, waits for them, and re-layouts, local(): rows_here = row_slabs[flavour, sector]  3.05 us
  transfers between devices with their start and end apart: 2, of which 1 were waited for; matrix products, arithmetic and copies ran while one was open for 19% of the time, Pallas kernels for 0%

profile of v1, /device:TPU:88, one launch (start us, length us, event | category | flops | bytes accessed | tf_op | source)
XLA Modules:
  0.0 84.0 jit_solution(8844779413349439218)
XLA Ops:
  0.2 2.6 %fusion.159 = bf16[1,1024,256]{2,1,0:T(8,128)(2,1)S(1)} fusion(bf16[2,1024,1024]{2,1,0:T(8,128)(2,1)} %param.15, bf16[3,2,1024,256]{3,2,1,0:T(8,128)(2,1)} %param.16), kind=kOutput, calls=%fused_computation.100 | convolution fusion | flops 537133056 | bytes 3145728 | tf_op jit(solution)/shard_map/dot_general | solution.py:21
  3.0 1.0 %copy-done.3 = bf16[3,2,1024,256]{3,2,1,0:T(8,128)(2,1)S(1)} copy-done((bf16[3,2,1024,256]{3,2,1,0:T(8,128)(2,1)S(1)}, bf16[3,2,1024,256]{3,2,1,0:T(8,128)(2,1)}, u32[]{:S(2)}) %copy-start.3) | copy-done | bytes 3145752
  4.0 0.8 fusion.162
  4.7 0.8 fusion.168
  5.5 0.8 fusion.156
  6.3 0.8 fusion.165
  7.2 0.8 fusion.171
  8.2 0.3 pad_maximum_fusion
  8.5 0.2 slice_bitcast_fusion.3
  8.8 1.9 %pad_maximum_fusion.1 = bf16[4,3,2,256,256]{4,3,2,1,0:T(8,128)(2,1)} fusion(bf16[1,3,2,256,256]{4,3,2,1,0:T(8,128)(2,1)S(1)} %get-tuple-element.186, bf16[1,3,2,256,256]{4,3,2,1,0:T(8,128)(2,1)S(1)} %get-tuple-element.187, bf16[1,3,2,256,256]{4,3,2,1,0:T(8,128)(2,1)S(1)} %get-tuple-element.188, bf16[1,3,2,256,256]{4,3,2,1,0:T(8,128)(2,1)S(1)} %get-tuple-element.185), kind=kLoop, calls=%fused_computation.73 | loop fusion | flops 4718592 | bytes 6291456 | tf_op jit(solution)/shard_map/stack | solution.py:9
  10.6 4.4 %all-to-all-start = ((bf16[4,3,2,256,256]{4,3,2,1,0:T(8,128)(2,1)}), bf16[4,3,2,256,256]{4,3,2,1,0:T(8,128)(2,1)S(1)}, u32[]{:S(2)}, u32[]{:S(2)}) async-start(bf16[4,3,2,256,256]{4,3,2,1,0:T(8,128)(2,1)} %pad_maximum_fusion.1), calls=%async_computation | async-start | bytes 6291456 | tf_op jit(solution)/shard_map/all_to_all | solution.py:10
  15.1 0.7 fusion.187
  19.4 33.2 %all-to-all-done = bf16[4,3,2,256,256]{4,3,2,1,0:T(8,128)(2,1)S(1)} async-done(((bf16[4,3,2,256,256]{4,3,2,1,0:T(8,128)(2,1)}), bf16[4,3,2,256,256]{4,3,2,1,0:T(8,128)(2,1)S(1)}, u32[]{:S(2)}, u32[]{:S(2)}) %all-to-all-start) | async-done | bytes 3145760 | tf_op jit(solution)/shard_map/all_to_all | solution.py:10
  52.6 2.8 %copy.10 = bf16[3,2,256,4,256]{2,4,3,1,0:T(8,128)(2,1)} copy(bf16[3,2,256,4,256]{4,2,1,0,3:T(8,128)(2,1)S(1)} %bitcast.252) | data formatting | bytes 6291456 | tf_op jit(solution)/shard_map/reshape | solution.py:11
  55.4 3.0 %slice_bitcast_fusion.9 = (bf16[256,1024]{0,1:T(8,128)(2,1)S(1)}, bf16[256,1024]{0,1:T(8,128)(2,1)}, bf16[256,1024]{0,1:T(8,128)(2,1)}, bf16[256,1024]{0,1:T(8,1...) fusion(bf16[3,2,256,1024]{2,3,1,0:T(8,128)(2,1)} %bitcast.253), kind=kLoop, calls=%fused_computation.120 | loop fusion | bytes 6291456 | tf_op jit(solution)/shard_map/squeeze | solution.py:46
  58.4 3.1 %conditional.6 = (bf16[1,256,1024]{2,1,0:T(8,128)(2,1)S(1)}) conditional(s32[]{:T(128)} %convert_element_type.114, (s32[]{:T(128)}, bf16[2,1024,1024]{2,1,0:T(8,128)(2,1)}, bf16[256,1024]{0,1:T(8,128)(2,1)S(1)}) %tuple.53, (s32[]{:T(128)}, bf16[2,1024,1024]{2,1,0:T(8,128)(2,1)}, bf16[256,1024]{0,1:T(8,128)(2,1)S(1)}) %tuple.54), branch_computations={%region_0.1_spmd, %region_1.2_spmd} | conditional | flops 537133056 | bytes 4194362 | solution.py:60
  59.0 2.4 %fusion.6 = bf16[1,256,1024]{1,2,0:T(8,128)(2,1)S(1)} fusion(bf16[256,1024]{0,1:T(8,128)(2,1)S(1)} %get-tuple-element.139, bf16[2,1024,1024]{2,1,0:T(8,128)(2,1)} %get-tuple-element.101, s32[]{:T(128)S(6)} %max.12), kind=kOutput, calls=%fused_computation.4 | convolution fusion | flops 537133056 | bytes 3145732 | tf_op jit(solution)/shard_map/cond/branch_0_fun/dot_general | solution.py:58
  61.4 0.2 copy.41
  61.6 3.2 %conditional.7 = (bf16[1,256,1024]{2,1,0:T(8,128)(2,1)S(1)}) conditional(s32[]{:T(128)} %convert_element_type.121, (s32[]{:T(128)}, bf16[2,1024,1024]{2,1,0:T(8,128)(2,1)}, bf16[256,1024]{0,1:T(8,128)(2,1)S(1)}) %tuple.55, (s32[]{:T(128)}, bf16[2,1024,1024]{2,1,0:T(8,128)(2,1)}, bf16[256,1024]{0,1:T(8,128)(2,1)S(1)}) %tuple.56), branch_computations={%region_2.3_spmd, %region_3.4_spmd} | conditional | flops 537133056 | bytes 4194362 | solution.py:60
  62.2 2.4 %fusion.26 = bf16[1,256,1024]{1,2,0:T(8,128)(2,1)S(1)} fusion(bf16[256,1024]{0,1:T(8,128)(2,1)S(1)} %get-tuple-element.145, bf16[2,1024,1024]{2,1,0:T(8,128)(2,1)} %get-tuple-element.107, s32[]{:T(128)S(6)} %max.13), kind=kOutput, calls=%fused_computation.16 | convolution fusion | flops 537133056 | bytes 3145732 | tf_op jit(solution)/shard_map/cond/branch_0_fun/dot_general | solution.py:58
  64.9 3.3 %conditional.8 = (bf16[1,256,1024]{2,1,0:T(8,128)(2,1)S(1)}) conditional(s32[]{:T(128)} %convert_element_type.122, (s32[]{:T(128)}, bf16[2,1024,1024]{2,1,0:T(8,128)(2,1)}, bf16[256,1024]{0,1:T(8,128)(2,1)S(1)}) %tuple.57, (s32[]{:T(128)}, bf16[2,1024,1024]{2,1,0:T(8,128)(2,1)}, bf16[256,1024]{0,1:T(8,128)(2,1)S(1)}) %tuple.58), branch_computations={%region_4.5_spmd, %region_5.6_spmd} | conditional | flops 537133056 | bytes 4194362 | solution.py:60
  65.7 2.4 %fusion.56 = bf16[1,256,1024]{1,2,0:T(8,128)(2,1)S(1)} fusion(bf16[256,1024]{0,1:T(8,128)(2,1)S(1)} %get-tuple-element.154, bf16[2,1024,1024]{2,1,0:T(8,128)(2,1)} %get-tuple-element.116, s32[]{:T(128)S(6)} %select_n.27), kind=kOutput, calls=%fused_computation.34 | convolution fusion | flops 537133056 | bytes 3145732 | tf_op jit(solution)/shard_map/cond/branch_1_fun/dot_general | solution.py:52
  68.3 3.2 %conditional.9 = (bf16[1,256,1024]{2,1,0:T(8,128)(2,1)S(1)}) conditional(s32[]{:T(128)} %convert_element_type.123, (s32[]{:T(128)}, bf16[2,1024,1024]{2,1,0:T(8,128)(2,1)}, bf16[256,1024]{0,1:T(8,128)(2,1)S(1)}) %tuple.59, (s32[]{:T(128)}, bf16[2,1024,1024]{2,1,0:T(8,128)(2,1)}, bf16[256,1024]{0,1:T(8,128)(2,1)S(1)}) %tuple.60), branch_computations={%region_6.7_spmd, %region_7.8_spmd} | conditional | flops 537133056 | bytes 4194362 | solution.py:60
  68.9 2.4 %fusion.66 = bf16[1,256,1024]{1,2,0:T(8,128)(2,1)S(1)} fusion(bf16[256,1024]{0,1:T(8,128)(2,1)S(1)} %get-tuple-element.157, bf16[2,1024,1024]{2,1,0:T(8,128)(2,1)} %get-tuple-element.119, s32[]{:T(128)S(6)} %max.15), kind=kOutput, calls=%fused_computation.40 | convolution fusion | flops 537133056 | bytes 3145732 | tf_op jit(solution)/shard_map/cond/branch_0_fun/dot_general | solution.py:58
  71.2 0.2 copy.47
  71.6 5.2 %conditional.10 = (bf16[1,256,1024]{2,1,0:T(8,128)(2,1)S(1)}) conditional(s32[]{:T(128)} %convert_element_type.124, (s32[]{:T(128)}, bf16[2,1024,1024]{2,1,0:T(8,128)(2,1)}, bf16[256,1024]{0,1:T(8,128)(2,1)}) %tuple.61, (s32[]{:T(128)}, bf16[2,1024,1024]{2,1,0:T(8,128)(2,1)}, bf16[256,1024]{0,1:T(8,128)(2,1)}) %tuple.62), branch_computations={%region_8.9_spmd, %region_9.10_spmd} | conditional | flops 537133056 | bytes 4194362 | solution.py:60
  72.3 3.2 %fusion.96 = bf16[1,256,1024]{1,2,0:T(8,128)(2,1)} fusion(bf16[256,1024]{0,1:T(8,128)(2,1)} %get-tuple-element.166, bf16[2,1024,1024]{2,1,0:T(8,128)(2,1)} %get-tuple-element.128, s32[]{:T(128)S(6)} %select_n.29), kind=kOutput, calls=%fused_computation.58 | convolution fusion | flops 537133056 | bytes 3145732 | tf_op jit(solution)/shard_map/cond/branch_1_fun/dot_general | solution.py:52
  75.5 1.2 %copy.50 = bf16[1,256,1024]{2,1,0:T(8,128)(2,1)S(1)} copy(bf16[1,256,1024]{1,2,0:T(8,128)(2,1)} %fusion.96) | data formatting | bytes 1048576 | tf_op jit(solution)/shard_map/cond | solution.py:60
  76.8 5.1 %conditional.11 = (bf16[1,256,1024]{2,1,0:T(8,128)(2,1)S(1)}) conditional(s32[]{:T(128)} %convert_element_type.125, (s32[]{:T(128)}, bf16[2,1024,1024]{2,1,0:T(8,128)(2,1)}, bf16[256,1024]{0,1:T(8,128)(2,1)S(1)}) %tuple.115, (s32[]{:T(128)}, bf16[2,1024,1024]{2,1,0:T(8,128)(2,1)}, bf16[256,1024]{0,1:T(8,128)(2,1)S(1)}) %tuple.116), branch_computations={%region_10.11_spmd, %region_11.12_spmd} | conditional | flops 537133056 | bytes 4194362 | solution.py:60
  77.5 3.2 %fusion.106 = bf16[1,256,1024]{1,2,0:T(8,128)(2,1)} fusion(bf16[256,1024]{0,1:T(8,128)(2,1)S(1)} %get-tuple-element.169, bf16[2,1024,1024]{2,1,0:T(8,128)(2,1)} %get-tuple-element.131, s32[]{:T(128)S(6)} %max.17), kind=kOutput, calls=%fused_computation.64 | convolution fusion | flops 537133056 | bytes 3145732 | tf_op jit(solution)/shard_map/cond/branch_0_fun/dot_general | solution.py:58
  80.6 1.2 %copy.51 = bf16[1,256,1024]{2,1,0:T(8,128)(2,1)S(1)} copy(bf16[1,256,1024]{1,2,0:T(8,128)(2,1)} %fusion.106) | data formatting | bytes 1048576 | tf_op jit(solution)/shard_map/cond | solution.py:60
  82.0 2.0 %pad_maximum_fusion.2 = bf16[3,2,256,1024]{3,2,1,0:T(8,128)(2,1)} fusion(bf16[1,2,256,1024]{3,2,1,0:T(8,128)(2,1)S(1)} %maximum_bitcast_fusion.5, bf16[1,2,256,1024]{3,2,1,0:T(8,128)(2,1)S(1)} %maximum_bitcast_fusion.4, bf16[1,2,256,1024]{3,2,1,0:T(8,128)(2,1)S(1)} %maximum_bitcast_fusion.3), kind=kLoop, calls=%fused_computation.74 | loop fusion | flops 3145728 | bytes 6291456 | tf_op jit(solution)/shard_map/stack | solution.py:63
  (17 shorter events, 1.4 us)
Async XLA Ops:
  0.0 3.0 %copy-start.2 = (bf16[2,1024,1024]{2,1,0:T(8,128)(2,1)S(1)}, bf16[2,1024,1024]{2,1,0:T(8,128)(2,1)}, u32[]{:S(2)}) copy-start(bf16[2,1024,1024]{2,1,0:T(8,128)(2,1)} %param.15) | copy-start | bytes 12582916
  0.0 4.0 %copy-start.3 = (bf16[3,2,1024,256]{3,2,1,0:T(8,128)(2,1)S(1)}, bf16[3,2,1024,256]{3,2,1,0:T(8,128)(2,1)}, u32[]{:S(2)}) copy-start(bf16[3,2,1024,256]{3,2,1,0:T(8,128)(2,1)} %param.16) | copy-start | bytes 9437188
  0.0 58.4 %collective-permute-start = (bf16[2,1024,1024]{2,1,0:T(8,128)(2,1)}, bf16[2,1024,1024]{2,1,0:T(8,128)(2,1)}, u32[]{:S(2)}, u32[]{:S(2)}) collective-permute-start(bf16[2,1024,1024]{2,1,0:T(8,128)(2,1)} %param.15), channel_id=1, source_target_pairs={{4,0},{8,4},{12,8},{16,12},{20,16},{24,20},{28,24},{32,28},{36,32}... | collective-permute-start | bytes 12582920 | tf_op jit(solution)/shard_map/ppermute | solution.py:17
  10.6 4.4 %copy-start.1 = (s32[3,2]{0,1:T(2,128)S(1)}, s32[3,2]{0,1:T(2,128)}, u32[]{:S(2)}) copy-start(s32[3,2]{0,1:T(2,128)} %param.17) | copy-start | bytes 76
  10.6 42.0 %all-to-all-start = ((bf16[4,3,2,256,256]{4,3,2,1,0:T(8,128)(2,1)}), bf16[4,3,2,256,256]{4,3,2,1,0:T(8,128)(2,1)S(1)}, u32[]{:S(2)}, u32[]{:S(2)}) async-start(bf16[4,3,2,256,256]{4,3,2,1,0:T(8,128)(2,1)} %pad_maximum_fusion.1), calls=%async_computation | async-start | bytes 6291456 | tf_op jit(solution)/shard_map/all_to_all | solution.py:10
  71.6 5.2 %copy-start = (bf16[256,1024]{0,1:T(8,128)(2,1)S(1)}, bf16[256,1024]{0,1:T(8,128)(2,1)}, u32[]{:S(2)}) copy-start(bf16[256,1024]{0,1:T(8,128)(2,1)} %get-tuple-element.180) | copy-start | bytes 1572868
